TPU v7x, 32 devices: a whole 2x2x4 slice. The times are simulated.
32 devices in a mesh: seg: 4 (over y, core), dp: 8 (over z, x).
Axes of the slice: x: 2, y: 2, z: 4, core: 2. Of those that a mesh axis runs over, the one named last changes fastest.
Arguments:
- queries: bfloat16 [8, 512, 2048], P('dp', 'seg'), may hold values from -32 to 32
- keys: bfloat16 [8, 512, 2048], P('dp', 'seg'), may hold values from -6 to 6
- values: bfloat16 [8, 512, 2048], P('dp', 'seg'), may hold values from -6 to 6
- rel_keys: bfloat16 [256, 2048], replicated, may hold values from -6 to 6
- bias_u: float32 [2048], replicated, may hold values from -3 to 3
- bias_v: float32 [2048], replicated, may hold values from -3 to 3
- d_out: bfloat16 [8, 512, 2048], P('dp', 'seg'), may hold values from -6 to 6
Outputs:
- d_queries: bfloat16 [8, 512, 2048], P('dp', 'seg')
- d_keys: bfloat16 [8, 512, 2048], P('dp', 'seg')
- d_rel_keys: float32 [256, 2048], P('seg', 'dp')
- d_bias_u: float32 [2048], replicated
- d_bias_v: float32 [2048], replicated
All inputs are finite; a program needn't handle non-finite values.
Results may differ from a plain program's by a relative error of at most 0.0068.
Values may be sent and summed in bfloat16 or wider, within the bound.
No kernel may reach another device: no remote copies, remote signals or barrier semaphores. Data moves between devices by JAX's collectives and lax.ppermute only.
A program may use at most 64 MiB of HBM per device.

v0:
```python
import jax
import jax.numpy as jnp
from jax import lax
from jax.sharding import PartitionSpec as P

DH = 128


def from_behind(block, axis, distance):
    devices = range(lax.axis_size(axis))
    route = [(i - distance, i) for i in devices if i - distance in devices]
    return lax.ppermute(block, axis, route)


def product(form, left, right):
    return jnp.einsum(form, left, right, preferred_element_type=jnp.float32)


def shift_rel(raw_scores):
    head_count, seg_rows, key_count = raw_scores.shape
    padded = jnp.pad(raw_scores, ((0, 0), (0, 0), (1, 0)))
    folded = padded.reshape(head_count, key_count + 1, seg_rows)[:, 1:, :]
    return folded.reshape(head_count, seg_rows, key_count)


def local_grads(
    query_rows,
    key_local,
    value_local,
    key_memory,
    value_memory,
    rel_keys,
    bias_u,
    bias_v,
    d_out,
    mem_on,
):
    seg_rows = query_rows.shape[0]
    mem_len = key_memory.shape[0]
    key_count = seg_rows + mem_len
    head_count = query_rows.shape[1] // DH
    keys_all = jnp.concatenate([key_memory, key_local], 0).reshape(key_count, head_count, DH)
    values_all = jnp.concatenate([value_memory, value_local], 0).reshape(key_count, head_count, DH)
    rel_heads = rel_keys.reshape(key_count, head_count, DH)
    query_wide = query_rows.astype(jnp.float32)
    q_content = (query_wide + bias_u).astype(jnp.bfloat16).reshape(seg_rows, head_count, DH)
    q_position = (query_wide + bias_v).astype(jnp.bfloat16).reshape(seg_rows, head_count, DH)
    content = product("ihd,jhd->hij", q_content, keys_all)
    position = shift_rel(product("ihd,phd->hip", q_position, rel_heads))
    score_scale = DH ** (-0.5)
    row_index = jnp.arange(seg_rows, dtype=jnp.int32)[:, None]
    key_index = jnp.arange(key_count, dtype=jnp.int32)[None, :]
    allowed = (key_index <= row_index + mem_len) & ((key_index >= mem_len) | mem_on)
    scores = jnp.where(allowed[None], score_scale * (content + position), -1e30)
    row_max = jnp.max(scores, axis=-1, keepdims=True)
    raised = jnp.exp(scores - row_max)
    weights = raised / jnp.sum(raised, axis=-1, keepdims=True)
    d_heads = d_out.reshape(seg_rows, head_count, DH)
    d_weights = product("ihd,jhd->hij", d_heads, values_all)
    centred = d_weights - jnp.sum(weights * d_weights, axis=-1, keepdims=True)
    grad_scores = (score_scale * weights * centred).astype(jnp.bfloat16)
    d_content = product("hij,jhd->ihd", grad_scores, keys_all)
    d_keys = product("hij,ihd->jhd", grad_scores[:, :, mem_len:], q_content)
    zero_raw = jnp.zeros((head_count, seg_rows, key_count), jnp.bfloat16)
    unshift = jax.vjp(shift_rel, zero_raw)[1]
    grad_rel = unshift(grad_scores)[0]
    d_position = product("hip,phd->ihd", grad_rel, rel_heads)
    d_rel = product("hip,ihd->phd", grad_rel, q_position).reshape(key_count, head_count * DH)
    d_query = (d_content + d_position).reshape(seg_rows, head_count * DH).astype(jnp.bfloat16)
    d_key = d_keys.reshape(seg_rows, head_count * DH).astype(jnp.bfloat16)
    return (
        d_query,
        d_key,
        d_rel,
        jnp.sum(d_content, 0).reshape(-1),
        jnp.sum(d_position, 0).reshape(-1),
    )


def shards(queries, keys, values, rel_keys, bias_u, bias_v, d_out):
    seg_rows = queries.shape[1]
    mem_len = rel_keys.shape[0] - seg_rows
    memory = from_behind((keys[0, seg_rows - mem_len :], values[0, seg_rows - mem_len :]), "seg", 1)
    mem_on = lax.axis_index("seg") > 0
    d_query, d_key, d_rel, d_content, d_position = local_grads(
        queries[0],
        keys[0],
        values[0],
        memory[0],
        memory[1],
        rel_keys,
        bias_u,
        bias_v,
        d_out[0],
        mem_on,
    )
    bias_grads = lax.psum((d_content, d_position), ("seg", "dp"))
    shared = lax.psum_scatter(d_rel, "seg", scatter_dimension=0, tiled=True)
    shared = lax.psum_scatter(shared, "dp", scatter_dimension=1, tiled=True)
    return (d_query[None], d_key[None], shared, bias_grads[0], bias_grads[1])


def solution(mesh):
    placed = (
        P("dp", "seg", None),
        P("dp", "seg", None),
        P("dp", "seg", None),
        P(),
        P(),
        P(),
        P("dp", "seg", None),
    )
    return jax.shard_map(
        shards,
        mesh=mesh,
        in_specs=placed,
        out_specs=(P("dp", "seg", None), P("dp", "seg", None), P("seg", "dp"), P(), P()),
        check_vma=False,
    )
```

profile of v0, /device:TPU:0, one launch (start us, length us, event | category | flops | bytes accessed | tf_op | source)
XLA Modules:
  0.0 174.5 jit_solution(12217957348637252360)
XLA Ops:
  7.2 2.1 %copy.33 = bf16[1,128,2048]{1,2,0:T(8,128)(2,1)} copy(bf16[1,128,2048]{2,1,0:T(8,128)(2,1)} %param.9) | data formatting | bytes 1048576 | tf_op args[2]
  9.4 3.2 %collective-permute-start.1 = (bf16[128,2048]{0,1:T(8,128)(2,1)}, bf16[128,2048]{0,1:T(8,128)(2,1)}, u32[]{:S(2)}, u32[]{:S(2)}) collective-permute-start(bf16[128,2048]{0,1:T(8,128)(2,1)} %bitcast.5), channel_id=1, source_target_pairs={{0,8},{8,16},{16,24},{1,9},{9,17},{17,25},{2,10},{10,18},{18,26},{... | collective-permute-start | bytes 1572872 | tf_op jit(solution)/shard_map/ppermute | solution.py:12
  12.5 2.0 %copy.24 = bf16[1,128,2048]{1,2,0:T(8,128)(2,1)} copy(bf16[1,128,2048]{2,1,0:T(8,128)(2,1)} %param.8) | data formatting | bytes 1048576 | tf_op args[1]
  14.6 4.7 %collective-permute-start = (bf16[128,2048]{0,1:T(8,128)(2,1)}, bf16[128,2048]{0,1:T(8,128)(2,1)}, u32[]{:S(2)}, u32[]{:S(2)}) collective-permute-start(bf16[128,2048]{0,1:T(8,128)(2,1)} %bitcast), channel_id=1, source_target_pairs={{0,8},{8,16},{16,24},{1,9},{9,17},{17,25},{2,10},{10,18},{18,26},{... | collective-permute-start | bytes 1572872 | tf_op jit(solution)/shard_map/ppermute | solution.py:12
  20.9 2.6 %pad.12 = f32[16,128,257]{2,1,0:T(8,128)} pad(f32[16,128,256]{2,1,0:T(8,128)S(1)} %fusion.15, f32[]{:T(128)} %constant.4.clone.1), padding=0_0x0_0x1_0 | pad | bytes 4202500 | tf_op jit(solution)/shard_map/jit(_pad)/pad | solution.py:21
  23.4 4.7 %reshape.134 = f32[16,257,128]{2,1,0:T(8,128)} reshape(f32[16,128,257]{2,1,0:T(8,128)} %pad.12) | data formatting | bytes 4210688 | tf_op jit(solution)/shard_map/reshape | solution.py:22
  28.1 3.2 %slice.9 = f32[16,256,128]{2,1,0:T(8,128)} slice(f32[16,257,128]{2,1,0:T(8,128)} %reshape.134), slice={[0:16], [1:257], [0:128]} | slice | bytes 4194304 | tf_op jit(solution)/shard_map/slice | solution.py:22
  31.3 2.9 %reshape.135 = f32[16,128,256]{2,1,0:T(8,128)} reshape(f32[16,256,128]{2,1,0:T(8,128)} %slice.9) | data formatting | bytes 4194304 | tf_op jit(solution)/shard_map/reshape | solution.py:23
  36.6 2.0 %copy.27 = bf16[128,16,128]{2,0,1:T(8,128)(2,1)} copy(bf16[128,16,128]{0,2,1:T(8,128)(2,1)} %bitcast.2) | data formatting | bytes 1048576 | tf_op jit(solution)/shard_map/concatenate | solution.py:42
  38.8 2.0 %copy.35 = bf16[128,16,128]{2,0,1:T(8,128)(2,1)} copy(bf16[128,16,128]{0,2,1:T(8,128)(2,1)} %bitcast.6) | data formatting | bytes 1048576 | tf_op jit(solution)/shard_map/concatenate | solution.py:43
  40.9 2.0 %copy.26 = bf16[128,16,128]{2,0,1:T(8,128)(2,1)} copy(bf16[128,16,128]{0,2,1:T(8,128)(2,1)} %bitcast.1) | data formatting | bytes 1048576 | tf_op jit(solution)/shard_map/concatenate | solution.py:42
  42.9 2.8 %fusion.6 = f32[16,256,128]{1,2,0:T(8,128)} fusion(bf16[128,16,128]{2,0,1:T(8,128)(2,1)S(1)} %copy.36, bf16[128,16,128]{2,0,1:T(8,128)(2,1)} %copy.35, bf16[128,16,128]{2,1,0:T(8,128)(2,1)S(1)} %bitcast.45), kind=kOutput, calls=%fused_computation.14 | convolution fusion | flops 136314880 | bytes 3670016 | tf_op jit(solution)/shard_map/ihd,jhd->hij/dot_general | solution.py:16
  45.7 5.4 %fusion.2 = (f32[16,128]{1,0:T(8,128)S(1)}, f32[16,128,256]{2,1,0:T(8,128)}) fusion(f32[16,256,128]{1,2,0:T(8,128)} %fusion.6, f32[16,128,256]{2,1,0:T(8,128)} %reshape.135, pred[128,256]{1,0:T(8,128)(4,1)S(1)} %fusion.16, bf16[128,16,128]{2,0,1:T(8,128)(2,1)} %copy.27, bf16[128,16,128]{2,0,1:T(8,128)(2,1)} %copy.26, f32[128,16,128]{0,2,1:T(8,128)S(1)} %bitcast.39, ...), kind=kOutput, calls=%fused_computation.4 | convolution fusion | flops 140511744 | bytes 8437760 | tf_op jit(solution)/shard_map/div | solution.py:57
  51.2 2.6 %fusion.4 = bf16[16,128,256]{2,1,0:T(8,128)(2,1)S(1)} fusion(f32[16,256,128]{1,2,0:T(8,128)} %fusion.6, f32[16,128,256]{2,1,0:T(8,128)} %get-tuple-element.21, f32[16,128]{1,0:T(8,128)S(1)} %get-tuple-element.20), kind=kLoop, calls=%fused_computation.6 | loop fusion | flops 2097152 | bytes 5251072 | tf_op jit(solution)/shard_map/convert_element_type | solution.py:61
  54.9 2.5 %pad.13 = bf16[16,257,128]{2,1,0:T(8,128)(2,1)} pad(bf16[16,256,128]{2,1,0:T(8,128)(2,1)} %reshape.136, bf16[]{:T(256)} %constant.22.clone.1), padding=0_0x1_0x0_0 | pad | bytes 2101250 | tf_op jit(solution)/shard_map/transpose(jvp())/pad | solution.py:22
  57.4 5.0 %reshape.137 = bf16[16,128,257]{2,1,0:T(8,128)(2,1)} reshape(bf16[16,257,128]{2,1,0:T(8,128)(2,1)} %pad.13) | data formatting | bytes 2105344 | tf_op jit(solution)/shard_map/transpose(jvp())/reshape | solution.py:22
  62.5 3.6 %fusion.10 = f32[16,128,256]{2,1,0:T(8,128)} fusion(bf16[16,128,257]{2,1,0:T(8,128)(2,1)} %reshape.137, f32[128,16,128]{0,2,1:T(8,128)S(1)} %bitcast.40, f32[16,128]{1,0:T(8,128)S(1)} %bitcast.50), kind=kOutput, calls=%fused_computation.21 | convolution fusion | flops 134742016 | bytes 4202496 | tf_op jit(solution)/shard_map/hip,ihd->phd/dot_general | solution.py:16
  66.1 2.9 %copy.41 = f32[256,2048]{1,0:T(8,128)} copy(f32[256,2048]{0,1:T(8,128)} %bitcast.44) | data formatting | bytes 4194304 | tf_op jit(solution)/shard_map/reshape | solution.py:68
  69.2 31.7 %reduce-scatter.3.cloned.1.call-done = f32[64,2048]{1,0:T(8,128)} async-done(((f32[256,2048]{1,0:T(8,128)}), f32[64,2048]{1,0:T(8,128)}) %reduce-scatter.3.cloned.1.call-update) | async-done | bytes 524304 | tf_op jit(solution)/shard_map/reduce_scatter | solution.py:98
  100.9 1.8 %convolution_bitcast_fusion.1 = f32[128,16,128]{0,2,1:T(8,128)S(1)} fusion(bf16[16,128,256]{2,1,0:T(8,128)(2,1)S(1)} %fusion.4, bf16[128,16,128]{2,0,1:T(8,128)(2,1)} %copy.27, bf16[128,16,128]{2,0,1:T(8,128)(2,1)} %copy.26), kind=kOutput, calls=%fused_computation.11 | convolution fusion | flops 136314880 | bytes 3145728 | tf_op jit(solution)/shard_map/hij,jhd->ihd/dot_general | solution.py:16
  102.7 1.4 fusion.21
  104.0 2.0 %copy.42 = bf16[1,128,2048]{2,1,0:T(8,128)(2,1)} copy(bf16[1,128,2048]{1,2,0:T(8,128)(2,1)} %bitcast.46) | data formatting | bytes 1048576
  107.6 39.6 %all-reduce.2 = (f32[2048]{0:T(1024)}, f32[2048]{0:T(1024)}) all-reduce(f32[2048]{0:T(1024)S(1)} %bitcast.52, f32[2048]{0:T(1024)S(1)} %bitcast.51), channel_id=1, replica_groups=mesh['seg'=4,'dp'=8] {'seg','dp'}, use_global_device_ids=true, to_apply=%region_6.7 | all-reduce | flops 4096 | bytes 32768 | tf_op jit(solution)/shard_map/psum | solution.py:97
  147.2 20.5 %reduce-scatter.5.cloned.1.call-done = f32[64,256]{1,0:T(8,128)} async-done(((f32[64,2048]{1,0:T(8,128)}), f32[64,256]{1,0:T(8,128)}) %reduce-scatter.5.cloned.1.call-update) | async-done | bytes 65552 | tf_op jit(solution)/shard_map/reduce_scatter | solution.py:99
  (27 shorter events, 7.1 us)
Async XLA Ops:
  7.2 12.1 %copy-start.2 = (bf16[1,128,2048]{2,1,0:T(8,128)(2,1)S(1)}, bf16[1,128,2048]{2,1,0:T(8,128)(2,1)}, u32[]{:S(2)}) copy-start(bf16[1,128,2048]{2,1,0:T(8,128)(2,1)} %param.7) | copy-start | bytes 1572868
  7.2 12.3 %copy-start.1 = (bf16[256,2048]{1,0:T(8,128)(2,1)S(1)}, bf16[256,2048]{1,0:T(8,128)(2,1)}, u32[]{:S(2)}) copy-start(bf16[256,2048]{1,0:T(8,128)(2,1)} %param.10) | copy-start | bytes 3145732
  7.2 93.7 %reduce-scatter.3.cloned.1.call-start = ((), (), s32[]{:S(2)}) async-start(), calls=%async_computation.2 | async-start | bytes 2621440 | tf_op jit(solution)/shard_map/reduce_scatter | solution.py:98
  9.4 29.4 %collective-permute-start.1 = (bf16[128,2048]{0,1:T(8,128)(2,1)}, bf16[128,2048]{0,1:T(8,128)(2,1)}, u32[]{:S(2)}, u32[]{:S(2)}) collective-permute-start(bf16[128,2048]{0,1:T(8,128)(2,1)} %bitcast.5), channel_id=1, source_target_pairs={{0,8},{8,16},{16,24},{1,9},{9,17},{17,25},{2,10},{10,18},{18,26},{... | collective-permute-start | bytes 1572872 | tf_op jit(solution)/shard_map/ppermute | solution.py:12
  14.6 5.4 %copy-start.3 = (f32[2048]{0:T(1024)S(1)}, f32[2048]{0:T(1024)}, u32[]{:S(2)}) copy-start(f32[2048]{0:T(1024)} %param.12) | copy-start | bytes 24580
  14.6 26.3 %collective-permute-start = (bf16[128,2048]{0,1:T(8,128)(2,1)}, bf16[128,2048]{0,1:T(8,128)(2,1)}, u32[]{:S(2)}, u32[]{:S(2)}) collective-permute-start(bf16[128,2048]{0,1:T(8,128)(2,1)} %bitcast), channel_id=1, source_target_pairs={{0,8},{8,16},{16,24},{1,9},{9,17},{17,25},{2,10},{10,18},{18,26},{... | collective-permute-start | bytes 1572872 | tf_op jit(solution)/shard_map/ppermute | solution.py:12
  42.9 2.8 %copy-start.4 = (f32[2048]{0:T(1024)S(1)}, f32[2048]{0:T(1024)}, u32[]{:S(2)}) copy-start(f32[2048]{0:T(1024)} %param.11) | copy-start | bytes 24580
  69.0 98.7 %reduce-scatter.5.cloned.1.call-start = ((), (), s32[]{:S(2)}) async-start(), calls=%async_computation.3 | async-start | bytes 589824 | tf_op jit(solution)/shard_map/reduce_scatter | solution.py:99
  100.9 1.8 %copy-start = (bf16[16,128,257]{2,1,0:T(8,128)(2,1)S(1)}, bf16[16,128,257]{2,1,0:T(8,128)(2,1)}, u32[]{:S(2)}) copy-start(bf16[16,128,257]{2,1,0:T(8,128)(2,1)} %reshape.137) | copy-start | bytes 3158020
Sparse Core Ops, SparseCore 0:
  69.1 31.7 reduce-scatter.2
  105.1 62.5 reduce-scatter.4
where the time goes:
time: 175 us
  waiting for transfers between devices  52.2 us (30%)
  local copies, waits for them, and re-layouts  41.5 us (24%)
  blocking collectives  39.6 us (23%)
  matrix products  16.3 us (9%)
  between operations  14.2 us (8%)
  starting transfers between devices  8.1 us (5%)
  other arithmetic  2.66 us (2%)
    psum x1, blocking collectives, shards(): bias_grads = lax.psum((d_content, d_position), ('seg', 'dp'))  39.6 us
    reduce_scatter x1, waiting for transfers between devices, shards(): shared = lax.psum_scatter(d_rel, 'seg', scatter_dimension=0, tiled=True)  31.7 us
    reduce_scatter x1, waiting for transfers between devices, shards(): shared = lax.psum_scatter(shared, 'dp', scatter_dimension=1, tiled=True)  20.5 us
    dot_general x6, matrix products, product(): return jnp.einsum(form, left, right, preferred_element_type=jnp.float32)  10.9 us
    reshape x2, local copies, waits for them, and re-layouts, shift_rel(): folded = padded.reshape(head_count, key_count + 1, seg_rows)[:, 1:, :]  9.72 us
    unnamed x15, local copies, waits for them, and re-layouts  8.4 us
    ppermute x2, starting transfers between devices, from_behind(): return lax.ppermute(block, axis, route)  7.84 us
    div x1, matrix products, local_grads(): weights = raised / jnp.sum(raised, axis=-1, keepdims=True)  5.43 us
  transfers between devices with their start and end apart: 4, of which 2 were waited for; matrix products, arithmetic and copies ran while one was open for 17% of the time, Pallas kernels for 0%

commit v1 on v0

--- a/solution.py
+++ b/solution.py
@@ -94,7 +94,7 @@
         d_out[0],
         mem_on,
     )
-    bias_grads = lax.psum((d_content, d_position), ("seg", "dp"))
+    bias_grads = lax.psum(lax.psum((d_content, d_position), "seg"), "dp")
     shared = lax.psum_scatter(d_rel, "seg", scatter_dimension=0, tiled=True)
     shared = lax.psum_scatter(shared, "dp", scatter_dimension=1, tiled=True)
     return (d_query[None], d_key[None], shared, bias_grads[0], bias_grads[1])

time: 175 us -> 175 us (level)
  waiting for transfers between devices: 52.2 us -> 43.8 us
  blocking collectives: 39.6 us -> 47.9 us
    reduce_scatter x1, waiting for transfers between devices: 20.5 us -> 12.1 us  [shards(): shared = lax.psum_scatter(shared, 'dp', scatter_dimension=1, tiled=True)]
    psum x1 -> x2, blocking collectives: 39.6 us -> 47.9 us  [shards(): bias_grads = lax.psum(lax.psum((d_content, d_position), 'seg'), 'dp')]
where the time goes in v1:
time: 175 us; the launch traced here: 174 us
  blocking collectives  47.9 us (27%)
  waiting for transfers between devices  43.8 us (25%)
  local copies, waits for them, and re-layouts  41.5 us (24%)
  matrix products  16.3 us (9%)
  between operations  14.2 us (8%)
  starting transfers between devices  8.1 us (5%)
  other arithmetic  2.66 us (2%)
    psum x2, blocking collectives, shards(): bias_grads = lax.psum(lax.psum((d_content, d_position), 'seg'), 'dp')  47.9 us
    reduce_scatter x1, waiting for transfers between devices, shards(): shared = lax.psum_scatter(d_rel, 'seg', scatter_dimension=0, tiled=True)  31.7 us
    reduce_scatter x1, waiting for transfers between devices, shards(): shared = lax.psum_scatter(shared, 'dp', scatter_dimension=1, tiled=True)  12.1 us
    dot_general x6, matrix products, product(): return jnp.einsum(form, left, right, preferred_element_type=jnp.float32)  10.9 us
    reshape x2, local copies, waits for them, and re-layouts, shift_rel(): folded = padded.reshape(head_count, key_count + 1, seg_rows)[:, 1:, :]  9.72 us
    unnamed x15, local copies, waits for them, and re-layouts  8.4 us
    ppermute x2, starting transfers between devices, from_behind(): return lax.ppermute(block, axis, route)  7.84 us
    div x1, matrix products, local_grads(): weights = raised / jnp.sum(raised, axis=-1, keepdims=True)  5.43 us
  transfers between devices with their start and end apart: 4, of which 2 were waited for; matrix products, arithmetic and copies ran while one was open for 17% of the time, Pallas kernels for 0%

profile of v1, /device:TPU:0, one launch (start us, length us, event | category | flops | bytes accessed | tf_op | source)
XLA Modules:
  0.0 174.4 jit_solution(8944122766898694312)
XLA Ops:
  7.2 2.1 %copy.33 = bf16[1,128,2048]{1,2,0:T(8,128)(2,1)} copy(bf16[1,128,2048]{2,1,0:T(8,128)(2,1)} %param.9) | data formatting | bytes 1048576 | tf_op args[2]
  9.4 3.2 %collective-permute-start.1 = (bf16[128,2048]{0,1:T(8,128)(2,1)}, bf16[128,2048]{0,1:T(8,128)(2,1)}, u32[]{:S(2)}, u32[]{:S(2)}) collective-permute-start(bf16[128,2048]{0,1:T(8,128)(2,1)} %bitcast.5), channel_id=1, source_target_pairs={{0,8},{8,16},{16,24},{1,9},{9,17},{17,25},{2,10},{10,18},{18,26},{... | collective-permute-start | bytes 1572872 | tf_op jit(solution)/shard_map/ppermute | solution.py:12
  12.5 2.0 %copy.24 = bf16[1,128,2048]{1,2,0:T(8,128)(2,1)} copy(bf16[1,128,2048]{2,1,0:T(8,128)(2,1)} %param.8) | data formatting | bytes 1048576 | tf_op args[1]
  14.6 4.7 %collective-permute-start = (bf16[128,2048]{0,1:T(8,128)(2,1)}, bf16[128,2048]{0,1:T(8,128)(2,1)}, u32[]{:S(2)}, u32[]{:S(2)}) collective-permute-start(bf16[128,2048]{0,1:T(8,128)(2,1)} %bitcast), channel_id=1, source_target_pairs={{0,8},{8,16},{16,24},{1,9},{9,17},{17,25},{2,10},{10,18},{18,26},{... | collective-permute-start | bytes 1572872 | tf_op jit(solution)/shard_map/ppermute | solution.py:12
  20.9 2.6 %pad.12 = f32[16,128,257]{2,1,0:T(8,128)} pad(f32[16,128,256]{2,1,0:T(8,128)S(1)} %fusion.15, f32[]{:T(128)} %constant.4.clone.1), padding=0_0x0_0x1_0 | pad | bytes 4202500 | tf_op jit(solution)/shard_map/jit(_pad)/pad | solution.py:21
  23.4 4.7 %reshape.134 = f32[16,257,128]{2,1,0:T(8,128)} reshape(f32[16,128,257]{2,1,0:T(8,128)} %pad.12) | data formatting | bytes 4210688 | tf_op jit(solution)/shard_map/reshape | solution.py:22
  28.1 3.2 %slice.9 = f32[16,256,128]{2,1,0:T(8,128)} slice(f32[16,257,128]{2,1,0:T(8,128)} %reshape.134), slice={[0:16], [1:257], [0:128]} | slice | bytes 4194304 | tf_op jit(solution)/shard_map/slice | solution.py:22
  31.3 2.9 %reshape.135 = f32[16,128,256]{2,1,0:T(8,128)} reshape(f32[16,256,128]{2,1,0:T(8,128)} %slice.9) | data formatting | bytes 4194304 | tf_op jit(solution)/shard_map/reshape | solution.py:23
  36.6 2.0 %copy.27 = bf16[128,16,128]{2,0,1:T(8,128)(2,1)} copy(bf16[128,16,128]{0,2,1:T(8,128)(2,1)} %bitcast.2) | data formatting | bytes 1048576 | tf_op jit(solution)/shard_map/concatenate | solution.py:42
  38.8 2.0 %copy.35 = bf16[128,16,128]{2,0,1:T(8,128)(2,1)} copy(bf16[128,16,128]{0,2,1:T(8,128)(2,1)} %bitcast.6) | data formatting | bytes 1048576 | tf_op jit(solution)/shard_map/concatenate | solution.py:43
  40.9 2.0 %copy.26 = bf16[128,16,128]{2,0,1:T(8,128)(2,1)} copy(bf16[128,16,128]{0,2,1:T(8,128)(2,1)} %bitcast.1) | data formatting | bytes 1048576 | tf_op jit(solution)/shard_map/concatenate | solution.py:42
  42.9 2.8 %fusion.6 = f32[16,256,128]{1,2,0:T(8,128)} fusion(bf16[128,16,128]{2,0,1:T(8,128)(2,1)S(1)} %copy.36, bf16[128,16,128]{2,0,1:T(8,128)(2,1)} %copy.35, bf16[128,16,128]{2,1,0:T(8,128)(2,1)S(1)} %bitcast.45), kind=kOutput, calls=%fused_computation.14 | convolution fusion | flops 136314880 | bytes 3670016 | tf_op jit(solution)/shard_map/ihd,jhd->hij/dot_general | solution.py:16
  45.7 5.4 %fusion.2 = (f32[16,128]{1,0:T(8,128)S(1)}, f32[16,128,256]{2,1,0:T(8,128)}) fusion(f32[16,256,128]{1,2,0:T(8,128)} %fusion.6, f32[16,128,256]{2,1,0:T(8,128)} %reshape.135, pred[128,256]{1,0:T(8,128)(4,1)S(1)} %fusion.16, bf16[128,16,128]{2,0,1:T(8,128)(2,1)} %copy.27, bf16[128,16,128]{2,0,1:T(8,128)(2,1)} %copy.26, f32[128,16,128]{0,2,1:T(8,128)S(1)} %bitcast.39, ...), kind=kOutput, calls=%fused_computation.4 | convolution fusion | flops 140511744 | bytes 8437760 | tf_op jit(solution)/shard_map/div | solution.py:57
  51.2 2.6 %fusion.4 = bf16[16,128,256]{2,1,0:T(8,128)(2,1)S(1)} fusion(f32[16,256,128]{1,2,0:T(8,128)} %fusion.6, f32[16,128,256]{2,1,0:T(8,128)} %get-tuple-element.23, f32[16,128]{1,0:T(8,128)S(1)} %get-tuple-element.22), kind=kLoop, calls=%fused_computation.6 | loop fusion | flops 2097152 | bytes 5251072 | tf_op jit(solution)/shard_map/convert_element_type | solution.py:61
  54.9 2.5 %pad.13 = bf16[16,257,128]{2,1,0:T(8,128)(2,1)} pad(bf16[16,256,128]{2,1,0:T(8,128)(2,1)} %reshape.136, bf16[]{:T(256)} %constant.22.clone.1), padding=0_0x1_0x0_0 | pad | bytes 2101250 | tf_op jit(solution)/shard_map/transpose(jvp())/pad | solution.py:22
  57.4 5.0 %reshape.137 = bf16[16,128,257]{2,1,0:T(8,128)(2,1)} reshape(bf16[16,257,128]{2,1,0:T(8,128)(2,1)} %pad.13) | data formatting | bytes 2105344 | tf_op jit(solution)/shard_map/transpose(jvp())/reshape | solution.py:22
  62.5 3.6 %fusion.10 = f32[16,128,256]{2,1,0:T(8,128)} fusion(bf16[16,128,257]{2,1,0:T(8,128)(2,1)} %reshape.137, f32[128,16,128]{0,2,1:T(8,128)S(1)} %bitcast.40, f32[16,128]{1,0:T(8,128)S(1)} %bitcast.50), kind=kOutput, calls=%fused_computation.21 | convolution fusion | flops 134742016 | bytes 4202496 | tf_op jit(solution)/shard_map/hip,ihd->phd/dot_general | solution.py:16
  66.1 2.9 %copy.41 = f32[256,2048]{1,0:T(8,128)} copy(f32[256,2048]{0,1:T(8,128)} %bitcast.44) | data formatting | bytes 4194304 | tf_op jit(solution)/shard_map/reshape | solution.py:68
  69.2 31.7 %reduce-scatter.3.cloned.1.call-done = f32[64,2048]{1,0:T(8,128)} async-done(((f32[256,2048]{1,0:T(8,128)}), f32[64,2048]{1,0:T(8,128)}) %reduce-scatter.3.cloned.1.call-update) | async-done | bytes 524304 | tf_op jit(solution)/shard_map/reduce_scatter | solution.py:98
  100.9 1.8 %convolution_bitcast_fusion.1 = f32[128,16,128]{0,2,1:T(8,128)S(1)} fusion(bf16[16,128,256]{2,1,0:T(8,128)(2,1)S(1)} %fusion.4, bf16[128,16,128]{2,0,1:T(8,128)(2,1)} %copy.27, bf16[128,16,128]{2,0,1:T(8,128)(2,1)} %copy.26), kind=kOutput, calls=%fused_computation.11 | convolution fusion | flops 136314880 | bytes 3145728 | tf_op jit(solution)/shard_map/hij,jhd->ihd/dot_general | solution.py:16
  104.0 2.0 %copy.42 = bf16[1,128,2048]{2,1,0:T(8,128)(2,1)} copy(bf16[1,128,2048]{1,2,0:T(8,128)(2,1)} %bitcast.46) | data formatting | bytes 1048576
  107.6 10.5 %all-reduce.3 = (f32[2048]{0:T(1024)S(1)}, f32[2048]{0:T(1024)S(1)}) all-reduce(f32[2048]{0:T(1024)S(1)} %bitcast.52, f32[2048]{0:T(1024)S(1)} %bitcast.51), channel_id=1, replica_groups=mesh['seg'=4,'dp'=8] {'seg'}, use_global_device_ids=true, to_apply=%region_6.7 | all-reduce | flops 4096 | bytes 32768 | tf_op jit(solution)/shard_map/psum | solution.py:97
  118.1 37.4 %all-reduce.2 = (f32[2048]{0:T(1024)}, f32[2048]{0:T(1024)}) all-reduce(f32[2048]{0:T(1024)S(1)} %get-tuple-element.17, f32[2048]{0:T(1024)S(1)} %get-tuple-element.18), channel_id=1, replica_groups=mesh['seg'=4,'dp'=8] {'dp'}, use_global_device_ids=true, to_apply=%region_7.8 | all-reduce | flops 4096 | bytes 32768 | tf_op jit(solution)/shard_map/psum | solution.py:97
  155.5 12.1 %reduce-scatter.5.cloned.1.call-done = f32[64,256]{1,0:T(8,128)} async-done(((f32[64,2048]{1,0:T(8,128)}), f32[64,256]{1,0:T(8,128)}) %reduce-scatter.5.cloned.1.call-update) | async-done | bytes 65552 | tf_op jit(solution)/shard_map/reduce_scatter | solution.py:99
  (28 shorter events, 8.5 us)
Async XLA Ops:
  7.2 12.1 %copy-start.2 = (bf16[1,128,2048]{2,1,0:T(8,128)(2,1)S(1)}, bf16[1,128,2048]{2,1,0:T(8,128)(2,1)}, u32[]{:S(2)}) copy-start(bf16[1,128,2048]{2,1,0:T(8,128)(2,1)} %param.7) | copy-start | bytes 1572868
  7.2 12.3 %copy-start.1 = (bf16[256,2048]{1,0:T(8,128)(2,1)S(1)}, bf16[256,2048]{1,0:T(8,128)(2,1)}, u32[]{:S(2)}) copy-start(bf16[256,2048]{1,0:T(8,128)(2,1)} %param.10) | copy-start | bytes 3145732
  7.2 93.7 %reduce-scatter.3.cloned.1.call-start = ((), (), s32[]{:S(2)}) async-start(), calls=%async_computation.2 | async-start | bytes 2621440 | tf_op jit(solution)/shard_map/reduce_scatter | solution.py:98
  9.4 29.4 %collective-permute-start.1 = (bf16[128,2048]{0,1:T(8,128)(2,1)}, bf16[128,2048]{0,1:T(8,128)(2,1)}, u32[]{:S(2)}, u32[]{:S(2)}) collective-permute-start(bf16[128,2048]{0,1:T(8,128)(2,1)} %bitcast.5), channel_id=1, source_target_pairs={{0,8},{8,16},{16,24},{1,9},{9,17},{17,25},{2,10},{10,18},{18,26},{... | collective-permute-start | bytes 1572872 | tf_op jit(solution)/shard_map/ppermute | solution.py:12
  14.6 5.4 %copy-start.3 = (f32[2048]{0:T(1024)S(1)}, f32[2048]{0:T(1024)}, u32[]{:S(2)}) copy-start(f32[2048]{0:T(1024)} %param.12) | copy-start | bytes 24580
  14.6 26.3 %collective-permute-start = (bf16[128,2048]{0,1:T(8,128)(2,1)}, bf16[128,2048]{0,1:T(8,128)(2,1)}, u32[]{:S(2)}, u32[]{:S(2)}) collective-permute-start(bf16[128,2048]{0,1:T(8,128)(2,1)} %bitcast), channel_id=1, source_target_pairs={{0,8},{8,16},{16,24},{1,9},{9,17},{17,25},{2,10},{10,18},{18,26},{... | collective-permute-start | bytes 1572872 | tf_op jit(solution)/shard_map/ppermute | solution.py:12
  42.9 2.8 %copy-start.4 = (f32[2048]{0:T(1024)S(1)}, f32[2048]{0:T(1024)}, u32[]{:S(2)}) copy-start(f32[2048]{0:T(1024)} %param.11) | copy-start | bytes 24580
  69.0 98.6 %reduce-scatter.5.cloned.1.call-start = ((), (), s32[]{:S(2)}) async-start(), calls=%async_computation.3 | async-start | bytes 589824 | tf_op jit(solution)/shard_map/reduce_scatter | solution.py:99
  100.9 1.8 %copy-start = (bf16[16,128,257]{2,1,0:T(8,128)(2,1)S(1)}, bf16[16,128,257]{2,1,0:T(8,128)(2,1)}, u32[]{:S(2)}) copy-start(bf16[16,128,257]{2,1,0:T(8,128)(2,1)} %reshape.137) | copy-start | bytes 3158020
Sparse Core Ops, SparseCore 0:
  69.1 31.7 reduce-scatter.2
  105.1 62.3 reduce-scatter.4
